TPU v7x, 32 devices: a whole 2x2x4 slice. The times are simulated.
32 devices in a mesh: fourier: 8 (over y, x, core), mer: 4 (over z).
Axes of the slice: x: 2, y: 2, z: 4, core: 2. Of those that a mesh axis runs over, the one named last changes fastest.
Arguments:
- velocity: float32 [3, 256, 64, 1024], P(None, 'fourier', None, 'mer')
- metrics: float32 [4, 64, 1024], P(None, None, 'mer'), may hold values from -0.3 to 0.3
- lumped_mass: float32 [64, 1024], P(None, 'mer'), may hold values from 0.5 to 2
- element_ops: float32 [64, 64, 1024], P(None, None, 'mer'), may hold values from -0.75 to 0.75
- boundary_map: int32 [1024, 28], P('mer'), may hold values from 0 to 13311, as said below
- block_cols: int32 [104, 4], P('mer'), may hold values from 0 to 103, as said below
- schur_blocks: float32 [104, 4, 128, 128], P('mer'), may hold values from -0.25 to 0.25
Outputs:
- element_out: float32 [3, 256, 64, 1024], P(None, 'fourier', None, 'mer')
- boundary_out: float32 [3, 256, 13312], P(None, 'fourier', 'mer')
Inputs may be any that keep to these rules, and one draw needn't show every extreme that they name: `boundary_map`: every entry of an element of slab s (elements s * 256 to (s + 1) * 256 - 1) lies from s * 3328 to (s + 1) * 3328 + 127, and for the last slab below (s + 1) * 3328; both ends are taken in every slab. `block_cols`: entry s of row r differs from r by at most 2; entry 0 is r itself.
All inputs are finite; a program needn't handle non-finite values.
Results may differ from a plain program's by a relative error of at most 0.00014.
Values sent between devices are 32-bit elements; how exact they have to be, the bound alone decides.
No kernel may reach another device: no remote copies, remote signals or barrier semaphores. Data moves between devices by JAX's collectives and lax.ppermute only.
A program may use at most 192 MiB of HBM per device.

v0:
```python
import jax
import jax.numpy as jnp
import numpy as np
from jax import lax
from jax.sharding import PartitionSpec as P

PERIM = 28
K = 256
HB = 2
gauss_nodes = [
    -1.0,
    -0.8717401485096066,
    -0.5917001814331423,
    -0.2092992179024789,
    0.2092992179024789,
    0.5917001814331423,
    0.8717401485096066,
    1.0,
]
wave_scale = 1.0 / 32.0


def passed_along(value, axis, by):
    count = lax.axis_size(axis)
    pairs = [(i, i + by) for i in range(count) if 0 <= i + by < count]
    return lax.ppermute(value, axis, pairs)


def padded(value, sides, width):
    for axis, dim in sides:
        count, length = (lax.axis_size(axis), value.shape[dim])
        up = [(i, (i + 1) % count) for i in range(count - 1)]
        down = [(j, i) for i, j in up]
        last = lax.slice_in_dim(value, length - width, length, axis=dim)
        leading = lax.slice_in_dim(value, 0, width, axis=dim)
        before = lax.ppermute(last, axis, up)
        after = lax.ppermute(leading, axis, down)
        value = jnp.concatenate([before, value, after], axis=dim)
    return value


def node_tables():
    nodes = np.array(gauss_nodes)
    count = nodes.shape[0]
    barycentric = np.array(
        [1.0 / np.prod([nodes[i] - nodes[k] for k in range(count) if k != i]) for i in range(count)]
    )
    matrix = np.zeros((count, count))
    for i in range(count):
        for j in range(count):
            if i != j:
                matrix[i, j] = barycentric[j] / barycentric[i] / (nodes[i] - nodes[j])
        matrix[i, i] = -np.sum(matrix[i])
    return (np.kron(matrix, np.eye(count)), np.kron(np.eye(count), matrix))


def perimeter_points():
    points = [8 * a + b for a in range(8) for b in range(8) if a in (0, 7) or b in (0, 7)]
    return np.array(points, dtype=np.int32)


def spectral_tables(modes):
    planes = 3 * modes // 2
    index = np.arange(modes)
    wave = np.where(index == modes - 1, modes // 2, (index + 1) // 2)
    is_sine = (index % 2 == 0) & (index > 0) & (index < modes - 1)
    theta = 2.0 * np.pi * np.arange(planes) / planes
    angle = theta[:, None] * wave[None, :]
    basis = np.where(is_sine[None, :], np.sin(angle), np.cos(angle))
    deriv = wave_scale * wave[None, :] * np.where(is_sine[None, :], np.cos(angle), -np.sin(angle))
    weight = np.where(index == 0, 1.0, 2.0) / planes
    back = (basis * weight[None, :]).T
    return (basis, deriv, back, wave)


def per_device(velocity, metrics, lumped_mass, element_ops, boundary_map, block_cols, schur_blocks):
    high = lax.Precision.HIGHEST
    modes = velocity.shape[1]
    elems = velocity.shape[3]
    groups = lax.axis_size("fourier")
    sub_elems = elems // groups
    part = lax.axis_index("fourier")
    slab = lax.axis_index("mer")
    block_rows = schur_blocks.shape[0]
    block_size = schur_blocks.shape[2]
    owned_count = block_rows * block_size
    basis, deriv, back, wave = spectral_tables(K)
    forward_table = jnp.asarray(basis, jnp.float32)
    deriv_table = jnp.asarray(deriv, jnp.float32)
    back_table = jnp.asarray(back, jnp.float32)
    deriv_r_np, deriv_s_np = node_tables()
    deriv_r = jnp.asarray(deriv_r_np, jnp.float32)
    deriv_s = jnp.asarray(deriv_s_np, jnp.float32)
    incoming = lax.all_to_all(velocity, "fourier", split_axis=3, concat_axis=1, tiled=True)
    physical = jnp.einsum("jk,fkpe->fjpe", forward_table, incoming, precision=high)
    planes = physical[:3]
    grad_z = jnp.einsum("jk,fkpe->fjpe", deriv_table, incoming, precision=high)
    local_metrics = lax.dynamic_slice_in_dim(metrics, part * sub_elems, sub_elems, 2)
    along_r = jnp.einsum("qp,fjpe->fjqe", deriv_r, planes, precision=high)
    along_s = jnp.einsum("qp,fjpe->fjqe", deriv_s, planes, precision=high)
    grad_x = local_metrics[0] * along_r + local_metrics[2] * along_s
    grad_y = local_metrics[1] * along_r + local_metrics[3] * along_s
    advection = -(planes[0:1] * grad_x + planes[1:2] * grad_y + planes[2:3] * grad_z)
    projected = jnp.einsum("kj,fjpe->fkpe", back_table, advection, precision=high)
    returned = lax.all_to_all(projected, "fourier", split_axis=1, concat_axis=3, tiled=True)
    forcing = velocity + returned
    wave_all = jnp.asarray(wave, jnp.float32)
    local_wave = lax.dynamic_slice_in_dim(wave_all, part * modes, modes)
    helm = 1.0 + 4.0 * (local_wave / (K / 2)) ** 2
    element_out = jnp.einsum("ije,fkje->fkie", element_ops, forcing, precision=high)
    element_out = element_out + helm[None, :, None, None] * lumped_mass[None, None] * forcing
    perim = perimeter_points()
    values = element_out[:, :, perim, :]
    values = jnp.transpose(values, (3, 2, 0, 1)).reshape(elems * PERIM, 3 * modes)
    local_ids = boundary_map.reshape(-1) - slab * owned_count
    partial_sums = jax.ops.segment_sum(values, local_ids, num_segments=owned_count + block_size)
    partial_sums = partial_sums.T.reshape(3, modes, owned_count + block_size)
    reach_rows = HB * block_size
    owned = partial_sums[:, :, :owned_count]
    shared = partial_sums[:, :, owned_count:]
    arrived = passed_along(shared, "mer", 1)
    owned = owned.at[:, :, :block_size].add(arrived)
    extended = padded(owned, (("mer", 2),), reach_rows)
    blocked = extended.reshape(3 * modes, block_rows + 2 * HB, block_size)
    local_cols = block_cols - slab * block_rows + HB
    picked = blocked[:, local_cols, :]
    result = jnp.einsum("rsab,frsb->fra", schur_blocks, picked, precision=high)
    boundary_out = result.reshape(3, modes, owned_count)
    return (element_out, boundary_out)


def solution(mesh):
    in_specs = (
        P(None, "fourier", None, "mer"),
        P(None, None, "mer"),
        P(None, "mer"),
        P(None, None, "mer"),
        P("mer", None),
        P("mer", None),
        P("mer", None, None, None),
    )
    out_specs = (P(None, "fourier", None, "mer"), P(None, "fourier", "mer"))
    return jax.shard_map(
        per_device, mesh=mesh, in_specs=in_specs, out_specs=out_specs, check_vma=False
    )
```

profile of v0, /device:TPU:0, one launch (start us, length us, event | category | flops | bytes accessed | tf_op | source)
XLA Modules:
  0.0 565.5 jit_solution(6990238287051673647)
XLA Ops:
  0.6 12.7 %copy.110 = f32[3,32,64,256]{2,1,0,3:T(8,128)} copy(f32[3,32,64,256]{3,2,1,0:T(8,128)} %param.17) | data formatting | bytes 12582912 | tf_op args[0]
  13.4 12.6 %reshape.114 = f32[8,1,196608]{2,1,0:T(1,128)} reshape(f32[256,3,32,64]{3,2,1,0:T(8,128)} %bitcast.101) | data formatting | bytes 12582912
  26.0 5.3 all-to-all-start
  31.5 0.7 copy.103
  32.2 0.7 copy.102
  32.9 0.7 copy.101
  33.5 69.6 %all-to-all-done = f32[8,1,196608]{2,1,0:T(1,128)} async-done(((f32[8,1,196608]{2,1,0:T(1,128)}), f32[8,1,196608]{2,1,0:T(1,128)}, u32[]{:S(2)}, u32[]{:S(2)}) %all-to-all-start) | async-done | bytes 6291488 | tf_op jit(solution)/shard_map/all_to_all | solution.py:94
  103.2 0.6 broadcast.68
  103.7 19.7 %reduce.2 = f32[8,196608]{1,0:T(8,128)} reduce(f32[8,1,196608]{2,1,0:T(1,128)} %all-to-all-done, f32[]{:T(128)} %broadcast.68), dimensions={1}, to_apply=%all_to_all.26.reduce_sub_computation | reduce | bytes 12582916 | tf_op jit(solution)/shard_map/all_to_all | solution.py:94
  123.4 12.2 %reshape.115 = f32[256,3,32,64]{3,2,1,0:T(8,128)} reshape(f32[8,196608]{1,0:T(8,128)} %reduce.2) | data formatting | bytes 12582912
  135.6 20.4 %copy.99 = f32[3,8,32,64,32]{3,4,2,1,0:T(8,128)} copy(f32[3,8,32,64,32]{3,2,0,4,1:T(8,128)} %bitcast.104) | data formatting | bytes 12582912 | tf_op jit(solution)/shard_map/all_to_all | solution.py:94
  155.9 11.0 %copy.100 = f32[3,256,64,32]{1,2,3,0:T(8,128)} copy(f32[3,256,64,32]{2,3,1,0:T(8,128)} %bitcast.105) | data formatting | bytes 12582912 | tf_op jit(solution)/shard_map/all_to_all | solution.py:94
  167.0 13.4 %convolution_bitcast_fusion = f32[3,384,64,32]{1,2,3,0:T(8,128)S(1)} fusion(f32[384,256,1,1]{1,0,3,2:T(8,128)S(1)} %copy-done.3, f32[3,256,64,32]{1,2,3,0:T(8,128)} %copy.100), kind=kOutput, calls=%fused_computation.18 | convolution fusion | flops 7247757312 | bytes 16121856 | tf_op jit(solution)/shard_map/jk,fkpe->fjpe/dot_general | solution.py:95
  180.4 3.7 slice_bitcast_fusion.2
  184.1 2.9 copy-done
  186.9 11.4 %fusion.15 = f32[3,384,32,64]{1,3,2,0:T(8,128)} fusion(f32[3,384,64,32]{1,2,3,0:T(8,128)S(1)} %convolution_bitcast_fusion, f32[64,64,1,1]{1,0,3,2:T(8,128)S(1)} %copy-done.6), kind=kOutput, calls=%fused_computation.40 | convolution fusion | flops 1811939328 | bytes 18890752 | tf_op jit(solution)/shard_map/qp,fjpe->fjqe/dot_general | solution.py:99
  198.3 12.5 %fusion.16 = f32[384,3,64,32]{0,2,3,1:T(8,128)} fusion(f32[384,256,1,1]{1,0,3,2:T(8,128)S(1)} %copy-done.2, f32[3,256,64,32]{1,2,3,0:T(8,128)S(1)} %bitcast.103), kind=kOutput, calls=%fused_computation.41 | convolution fusion | flops 7247757312 | bytes 16121856 | tf_op jit(solution)/shard_map/jk,fkpe->fjpe/dot_general | solution.py:97
  210.8 21.6 %fusion = f32[3,384,64,32]{1,2,3,0:T(8,128)} fusion(f32[3,384,32,64]{1,3,2,0:T(8,128)} %fusion.15, f32[384,3,64,32]{0,2,3,1:T(8,128)} %fusion.16, f32[384,64,32]{0,1,2:T(8,128)} %get-tuple-element.25, f32[64,32]{0,1:T(8,128)S(1)} %copy.104, f32[64,32]{0,1:T(8,128)} %copy.103, f32[384,64,32]{0,1,2:T(8,128)} %get-tuple-element.26, f32[64,32]{0,1:T(8,128)} %copy.102, ...), kind=kOutput, calls=%fused_computation.6 | convolution fusion | flops 1840250880 | bytes 47235072 | tf_op jit(solution)/shard_map/qp,fjpe->fjqe/dot_general | solution.py:100
  232.5 20.0 %fusion.8 = f32[3,256,64,32]{1,3,2,0:T(8,128)} fusion(f32[256,384,1,1]{1,0,3,2:T(8,128)S(1)} %copy-done.1, f32[3,384,64,32]{1,2,3,0:T(8,128)} %fusion), kind=kOutput, calls=%fused_computation.22 | convolution fusion | flops 7247757312 | bytes 16121856 | tf_op jit(solution)/shard_map/kj,fjpe->fkpe/dot_general | solution.py:104
  252.5 12.8 %copy.107 = f32[3,256,64,32]{2,3,0,1:T(8,128)} copy(f32[3,256,64,32]{1,3,2,0:T(8,128)} %fusion.8) | data formatting | bytes 12582912 | tf_op jit(solution)/shard_map/kj,fjpe->fkpe/transpose | solution.py:104
  265.2 12.6 %reshape.116 = f32[8,1,196608]{2,1,0:T(1,128)} reshape(f32[256,3,32,64]{3,2,1,0:T(8,128)} %bitcast.106) | data formatting | bytes 12582912
  277.9 4.9 all-to-all-start.1
  283.0 9.2 %copy.127 = f32[64,64,256,1]{1,0,3,2:T(8,128)} copy(f32[64,64,256,1]{2,1,0,3:T(8,128)} %bitcast.114) | data formatting | bytes 8388608 | tf_op args[3]
  292.5 2.6 broadcast_multiply_fusion
  295.0 59.4 %all-to-all-done.1 = f32[8,1,196608]{2,1,0:T(1,128)} async-done(((f32[8,1,196608]{2,1,0:T(1,128)}), f32[8,1,196608]{2,1,0:T(1,128)}, u32[]{:S(2)}, u32[]{:S(2)}) %all-to-all-start.1) | async-done | bytes 6291488 | tf_op jit(solution)/shard_map/all_to_all | solution.py:105
  354.4 19.7 %reduce.3 = f32[8,196608]{1,0:T(8,128)} reduce(f32[8,1,196608]{2,1,0:T(1,128)} %all-to-all-done.1, f32[]{:T(128)} %broadcast.68), dimensions={1}, to_apply=%all_to_all.30.reduce_sub_computation | reduce | bytes 12582916 | tf_op jit(solution)/shard_map/all_to_all | solution.py:105
  374.1 12.3 %reshape.117 = f32[256,3,32,64]{3,2,1,0:T(8,128)} reshape(f32[8,196608]{1,0:T(8,128)} %reduce.3) | data formatting | bytes 12582912
  386.3 16.4 %copy.109 = f32[3,32,64,8,32]{2,1,0,4,3:T(8,128)} copy(f32[3,32,64,8,32]{2,4,0,1,3:T(8,128)} %bitcast.107) | data formatting | bytes 12582912 | tf_op jit(solution)/shard_map/all_to_all | solution.py:105
  402.7 14.6 %bitcast_add_fusion.1 = f32[3,32,64,256]{2,1,0,3:T(8,128)} fusion(f32[3,32,64,256]{2,1,0,3:T(8,128)} %copy.110, f32[3,32,64,8,32]{2,1,0,4,3:T(8,128)} %copy.109), kind=kLoop, calls=%fused_computation.4 | loop fusion | flops 1572864 | bytes 18874368 | tf_op jit(solution)/shard_map/add | solution.py:106
  417.3 25.5 %bitcast_add_fusion = f32[3,32,64,256]{2,1,0,3:T(8,128)} fusion(f32[3,32,64,256]{2,1,0,3:T(8,128)} %bitcast_add_fusion.1, f32[32,64,256]{1,0,2:T(8,128)} %broadcast_multiply_fusion, f32[64,64,256,1]{1,0,3,2:T(8,128)} %copy.127), kind=kOutput, calls=%fused_computation.3 | convolution fusion | flops 1211105280 | bytes 18874368 | tf_op jit(solution)/shard_map/ije,fkje->fkie/dot_general | solution.py:110
  442.9 12.1 %copy.114 = f32[3,32,64,256]{3,1,0,2:T(8,128)} copy(f32[3,32,64,256]{2,1,0,3:T(8,128)} %bitcast_add_fusion) | data formatting | bytes 12582912 | tf_op jit(solution)/shard_map/add | solution.py:111
  454.9 3.5 gather_fusion
  458.5 10.0 %copy.133 = f32[256,28,3,32]{3,2,1,0:T(4,128)} copy(f32[256,28,3,32]{0,3,2,1:T(8,128)S(1)} %bitcast.109) | data formatting | bytes 5505024 | tf_op jit(solution)/shard_map/reshape | solution.py:114
  468.4 14.7 %reshape.111 = f32[7168,96]{1,0:T(8,128)} reshape(f32[256,28,3,32]{3,2,1,0:T(4,128)} %copy.133) | data formatting | bytes 5505024 | tf_op jit(solution)/shard_map/reshape | solution.py:114
  483.1 39.3 %scatter_custom_fusion = f32[3456,96]{1,0:T(8,128)S(1)} fusion(s32[7168]{0:T(1024)S(1)} %reshape.95, f32[7168,96]{1,0:T(8,128)} %reshape.111, f32[]{:T(128)} %constant.71.clone.1), kind=kCustom, calls=%fused_computation.26 | custom fusion | flops 688128 | bytes 1327616 | tf_op jit(solution)/shard_map/scatter-add | solution.py:116
  522.5 0.5 copy.117
  523.0 4.4 collective-permute-start
  527.7 1.4 collective-permute-done
  529.1 1.5 collective-permute-start.2
  530.7 4.9 collective-permute-start.1
  535.6 11.0 %copy.121 = f32[3,32,64,256]{3,2,1,0:T(8,128)} copy(f32[3,32,64,256]{2,1,0,3:T(8,128)} %bitcast_add_fusion) | data formatting | bytes 12582912
  546.6 1.2 pad_maximum_fusion
  547.8 1.6 reshape.75
  549.4 0.9 copy.119
  550.3 3.1 gather_fusion.1
  553.4 9.8 %convolution_bitcast_fusion.1 = f32[96,26,128]{2,0,1:T(8,128)S(1)} fusion(f32[96,26,4,128]{3,0,2,1:T(8,128)} %bitcast.108, f32[26,4,128,128]{3,2,1,0:T(8,128)} %param.23), kind=kOutput, calls=%fused_computation.25 | convolution fusion | flops 1962934272 | bytes 13205504 | tf_op jit(solution)/shard_map/rsab,frsb->fra/dot_general | solution.py:127
  563.2 0.8 copy.120
  564.0 1.3 reshape.76
  (44 shorter events, 1.0 us)
Async XLA Ops:
  26.0 5.3 copy-start.5
  26.0 77.1 %all-to-all-start = ((f32[8,1,196608]{2,1,0:T(1,128)}), f32[8,1,196608]{2,1,0:T(1,128)}, u32[]{:S(2)}, u32[]{:S(2)}) async-start(f32[8,1,196608]{2,1,0:T(1,128)} %reshape.114), calls=%async_computation | async-start | bytes 12582912 | tf_op jit(solution)/shard_map/all_to_all | solution.py:94
  155.9 11.0 %copy-start.3 = (f32[384,256,1,1]{1,0,3,2:T(8,128)S(1)}, f32[384,256,1,1]{1,0,3,2:T(8,128)}, u32[]{:S(2)}) copy-start(f32[384,256,1,1]{1,0,3,2:T(8,128)} %constant.89) | copy-start | bytes 1179652
  180.3 6.6 %copy-start = (f32[3,384,64,32]{1,2,3,0:T(8,128)}, f32[3,384,64,32]{1,2,3,0:T(8,128)S(1)}, u32[]{:S(2)}) copy-start(f32[3,384,64,32]{1,2,3,0:T(8,128)S(1)} %convolution_bitcast_fusion) | copy-start | bytes 28311556
  180.4 6.6 %copy-start.6 = (f32[64,64,1,1]{1,0,3,2:T(8,128)S(1)}, f32[64,64,1,1]{1,0,3,2:T(8,128)}, u32[]{:S(2)}) copy-start(f32[64,64,1,1]{1,0,3,2:T(8,128)} %constant.90) | copy-start | bytes 49156
  180.4 17.9 %slice-start = ((s8[6291456]{0:T(1024)(128)(4,1)}), s8[4194304]{0:T(1024)(128)(4,1)S(1)}, s32[]{:S(2)}) async-start(s8[6291456]{0:T(1024)(128)(4,1)} %bitcast.102), calls=%async_computation.2 | async-start | bytes 8388608
  186.9 11.4 %slice-start.1 = ((s8[6291456]{0:T(1024)(128)(4,1)}), s8[2097152]{0:T(1024)(128)(4,1)S(1)}, s32[]{:S(2)}) async-start(s8[6291456]{0:T(1024)(128)(4,1)} %bitcast.102), calls=%async_computation.3 | async-start | bytes 4194304
  186.9 11.4 %copy-start.2 = (f32[384,256,1,1]{1,0,3,2:T(8,128)S(1)}, f32[384,256,1,1]{1,0,3,2:T(8,128)}, u32[]{:S(2)}) copy-start(f32[384,256,1,1]{1,0,3,2:T(8,128)} %constant.92) | copy-start | bytes 1179652
  210.8 21.7 %copy-start.1 = (f32[256,384,1,1]{1,0,3,2:T(8,128)S(1)}, f32[256,384,1,1]{1,0,3,2:T(8,128)}, u32[]{:S(2)}) copy-start(f32[256,384,1,1]{1,0,3,2:T(8,128)} %constant.93) | copy-start | bytes 1179652
  277.9 5.0 copy-start.4
  277.9 76.5 %all-to-all-start.1 = ((f32[8,1,196608]{2,1,0:T(1,128)}), f32[8,1,196608]{2,1,0:T(1,128)}, u32[]{:S(2)}, u32[]{:S(2)}) async-start(f32[8,1,196608]{2,1,0:T(1,128)} %reshape.116), calls=%async_computation.1 | async-start | bytes 12582912 | tf_op jit(solution)/shard_map/all_to_all | solution.py:105
  282.9 9.2 %copy-start.7 = (s32[256,28]{0,1:T(8,128)S(1)}, s32[256,28]{0,1:T(8,128)}, u32[]{:S(2)}) copy-start(s32[256,28]{0,1:T(8,128)} %param.21) | copy-start | bytes 86020
  282.9 9.4 %copy-start.10 = (f32[256]{0:T(256)S(1)}, f32[256]{0:T(256)}, u32[]{:S(2)}) copy-start(f32[256]{0:T(256)} %constant.82.clone) | copy-start | bytes 3076
  283.0 9.5 %copy-start.9 = (s32[28]{0:T(128)S(1)}, s32[28]{0:T(128)}, u32[]{:S(2)}) copy-start(s32[28]{0:T(128)} %constant.88) | copy-start | bytes 340
  468.4 58.9 %copy-start.8 = (s32[26,4]{0,1:T(4,128)S(1)}, s32[26,4]{0,1:T(4,128)}, u32[]{:S(2)}) copy-start(s32[26,4]{0,1:T(4,128)} %param.22) | copy-start | bytes 1252
  523.0 6.1 %collective-permute-start = (f32[3,32,128]{2,1,0:T(8,128)S(1)}, f32[3,32,128]{2,1,0:T(8,128)S(1)}, u32[]{:S(2)}, u32[]{:S(2)}) collective-permute-start(f32[3,32,128]{2,1,0:T(8,128)S(1)} %slice.79), channel_id=1, source_target_pairs={{0,1},{1,2},{2,3},{4,5},{5,6},{6,7},{8,9},{9,10},{10,11},{12,13},{... | collective-permute-start | bytes 147464 | tf_op jit(solution)/shard_map/ppermute | solution.py:26
  529.1 17.4 %collective-permute-start.2 = (f32[3,32,256]{2,1,0:T(8,128)S(1)}, f32[3,32,256]{2,1,0:T(8,128)S(1)}, u32[]{:S(2)}, u32[]{:S(2)}) collective-permute-start(f32[3,32,256]{2,1,0:T(8,128)S(1)} %get-tuple-element.28), channel_id=1, source_target_pairs={{1,0},{2,1},{3,2},{5,4},{6,5},{7,6},{9,8},{10,9},{11,10},{13,12},{... | collective-permute-start | bytes 294920 | tf_op jit(solution)/shard_map/ppermute | solution.py:37
  530.7 15.9 %collective-permute-start.1 = (f32[3,32,256]{2,1,0:T(8,128)S(1)}, f32[3,32,256]{2,1,0:T(8,128)S(1)}, u32[]{:S(2)}, u32[]{:S(2)}) collective-permute-start(f32[3,32,256]{2,1,0:T(8,128)S(1)} %get-tuple-element.27), channel_id=1, source_target_pairs={{0,1},{1,2},{2,3},{4,5},{5,6},{6,7},{8,9},{9,10},{10,11},{12,13},{... | collective-permute-start | bytes 294920 | tf_op jit(solution)/shard_map/ppermute | solution.py:36
where the time goes:
time: 571 us; the launch traced here: 566 us
  local copies, waits for them, and re-layouts  202 us (35%)
  waiting for transfers between devices  130 us (23%)
  matrix products  114 us (20%)
  other arithmetic  97.2 us (17%)
  starting transfers between devices  21 us (4%)
    unnamed x34, local copies, waits for them, and re-layouts  85.6 us
    all_to_all x1, waiting for transfers between devices, per_device(): lax.all_to_all(velocity, 'fourier', split_axis=3, concat_axis=1, tiled=True)  69.6 us
    all_to_all x1, waiting for transfers between devices, per_device(): lax.all_to_all(projected, 'fourier', split_axis=1, concat_axis=3, tiled=T...  59.4 us
    scatter-add x1, other arithmetic, per_device(): jax.ops.segment_sum(values, local_ids, num_segments=owned_count + block_s...  39.3 us
    all_to_all x3, local copies, waits for them, and re-layouts, per_device(): lax.all_to_all(velocity, 'fourier', split_axis=3, concat_axis=1, tiled=True)  32 us
    dot_general x1, matrix products, per_device(): jnp.einsum('ije,fkje->fkie', element_ops, forcing, precision=high)  25.5 us
    reshape x2, local copies, waits for them, and re-layouts, per_device(): jnp.transpose(values, (3, 2, 0, 1)).reshape(elems * PERIM, 3 * modes)  24.7 us
    dot_general x1, matrix products, per_device(): along_s = jnp.einsum('qp,fjpe->fjqe', deriv_s, planes, precision=high)  21.6 us
  transfers between devices with their start and end apart: 5, of which 3 were waited for; matrix products, arithmetic and copies ran while one was open for 5% of the time, Pallas kernels for 0%

commit v1 on v0

--- a/solution.py
+++ b/solution.py
@@ -102,7 +102,19 @@
     grad_y = local_metrics[1] * along_r + local_metrics[3] * along_s
     advection = -(planes[0:1] * grad_x + planes[1:2] * grad_y + planes[2:3] * grad_z)
     projected = jnp.einsum("kj,fjpe->fkpe", back_table, advection, precision=high)
-    returned = lax.all_to_all(projected, "fourier", split_axis=1, concat_axis=3, tiled=True)
+    ways, here = (lax.axis_size("fourier"), lax.axis_index("fourier"))
+    width_2 = projected.shape[1] // ways
+    lengths = list(projected.shape)
+    lengths[1] = width_2
+    height = lengths[3]
+    lengths[3] = height * ways
+    full = jnp.zeros(lengths, projected.dtype)
+    for mask in range(ways):
+        part_2 = lax.dynamic_slice_in_dim(projected, (here ^ mask) * width_2, width_2, axis=1)
+        if mask:
+            part_2 = lax.ppermute(part_2, "fourier", [(d, d ^ mask) for d in range(ways)])
+        full = lax.dynamic_update_slice_in_dim(full, part_2, (here ^ mask) * height, axis=3)
+    returned = full
     forcing = velocity + returned
     wave_all = jnp.asarray(wave, jnp.float32)
     local_wave = lax.dynamic_slice_in_dim(wave_all, part * modes, modes)

time: 571 us -> 602 us (1.054)
  waiting for transfers between devices: 130 us -> 174 us
  other arithmetic: 97.2 us -> 63 us
  local copies, waits for them, and re-layouts: 202 us -> 214 us
  matrix products: 114 us -> 124 us
    ppermute x0 -> x7, waiting for transfers between devices: none -> 101 us  [per_device(): lax.ppermute(part_2, 'fourier', [(d, d ^ mask) for d in range(ways)])]
    all_to_all x1 -> x0, waiting for transfers between devices: 59.4 us -> none  [per_device(): lax.all_to_all(projected, 'fourier', split_axis=1, concat_axis=3, tiled=T...]
    dynamic_slice x0 -> x9, local copies, waits for them, and re-layouts: none -> 39.4 us  [per_device(): lax.dynamic_slice_in_dim(projected, (here ^ mask) * width_2, width_2, axi...]
    unnamed x34 -> x44, local copies, waits for them, and re-layouts: 85.6 us -> 61.2 us
    dynamic_update_slice x0 -> x8, local copies, waits for them, and re-layouts: none -> 22.9 us  [per_device(): lax.dynamic_update_slice_in_dim(full, part_2, (here ^ mask) * height, axi...]
    all_to_all x1 -> x0, other arithmetic: 19.7 us -> none  [per_device(): lax.all_to_all(projected, 'fourier', split_axis=1, concat_axis=3, tiled=T...]
    all_to_all x1 -> x0, local copies, waits for them, and re-layouts: 16.4 us -> none  [per_device(): lax.all_to_all(projected, 'fourier', split_axis=1, concat_axis=3, tiled=T...]
    add x1 -> x0, other arithmetic: 14.6 us -> none  [per_device(): forcing = velocity + returned]
  transfers between devices with their start and end apart: 5 -> 11, of which waited for: 3 -> 4; matrix products, arithmetic and copies ran while one was open for 5% -> 12% of each run, Pallas kernels for 0% -> 0%
where the time goes in v1:
time: 602 us; the launch traced here: 597 us
  local copies, waits for them, and re-layouts  214 us (36%)
  waiting for transfers between devices  174 us (29%)
  matrix products  124 us (21%)
  other arithmetic  63 us (10%)
  starting transfers between devices  21.4 us (4%)
    ppermute x7, waiting for transfers between devices, per_device(): lax.ppermute(part_2, 'fourier', [(d, d ^ mask) for d in range(ways)])  101 us
    all_to_all x1, waiting for transfers between devices, per_device(): lax.all_to_all(velocity, 'fourier', split_axis=3, concat_axis=1, tiled=True)  71.2 us
    unnamed x44, local copies, waits for them, and re-layouts  61.2 us
    dynamic_slice x9, local copies, waits for them, and re-layouts, per_device(): lax.dynamic_slice_in_dim(projected, (here ^ mask) * width_2, width_2, axi...  39.4 us
    scatter-add x1, other arithmetic, per_device(): jax.ops.segment_sum(values, local_ids, num_segments=owned_count + block_s...  39.3 us
    dot_general x1, matrix products, per_device(): jnp.einsum('ije,fkje->fkie', element_ops, forcing, precision=high)  35.7 us
    all_to_all x3, local copies, waits for them, and re-layouts, per_device(): lax.all_to_all(velocity, 'fourier', split_axis=3, concat_axis=1, tiled=True)  31.7 us
    reshape x2, local copies, waits for them, and re-layouts, per_device(): jnp.transpose(values, (3, 2, 0, 1)).reshape(elems * PERIM, 3 * modes)  24.7 us
  transfers between devices with their start and end apart: 11, of which 4 were waited for; matrix products, arithmetic and copies ran while one was open for 12% of the time, Pallas kernels for 0%

profile of v1, /device:TPU:0, one launch (start us, length us, event | category | flops | bytes accessed | tf_op | source)
XLA Modules:
  0.0 597.1 jit_solution(2658565825616880431)
XLA Ops:
  0.6 12.8 %copy.116 = f32[3,32,64,256]{2,1,0,3:T(8,128)} copy(f32[3,32,64,256]{3,2,1,0:T(8,128)} %param.17) | data formatting | bytes 12582912 | tf_op args[0]
  13.4 12.6 %reshape.114 = f32[8,1,196608]{2,1,0:T(1,128)} reshape(f32[256,3,32,64]{3,2,1,0:T(8,128)} %bitcast.107) | data formatting | bytes 12582912
  26.0 5.3 all-to-all-start
  32.0 71.2 %all-to-all-done = f32[8,1,196608]{2,1,0:T(1,128)} async-done(((f32[8,1,196608]{2,1,0:T(1,128)}), f32[8,1,196608]{2,1,0:T(1,128)}, u32[]{:S(2)}, u32[]{:S(2)}) %all-to-all-start) | async-done | bytes 6291488 | tf_op jit(solution)/shard_map/all_to_all | solution.py:94
  103.7 19.7 %reduce.2 = f32[8,196608]{1,0:T(8,128)} reduce(f32[8,1,196608]{2,1,0:T(1,128)} %all-to-all-done, f32[]{:T(128)} %broadcast.68), dimensions={1}, to_apply=%all_to_all.13.reduce_sub_computation | reduce | bytes 12582916 | tf_op jit(solution)/shard_map/all_to_all | solution.py:94
  123.3 12.2 %reshape.115 = f32[256,3,32,64]{3,2,1,0:T(8,128)} reshape(f32[8,196608]{1,0:T(8,128)} %reduce.2) | data formatting | bytes 12582912
  135.5 20.2 %copy.93 = f32[3,8,32,64,32]{3,4,2,1,0:T(8,128)} copy(f32[3,8,32,64,32]{3,2,0,4,1:T(8,128)} %bitcast.110) | data formatting | bytes 12582912 | tf_op jit(solution)/shard_map/all_to_all | solution.py:94
  155.7 11.0 %copy.94 = f32[3,256,64,32]{1,2,3,0:T(8,128)} copy(f32[3,256,64,32]{2,3,1,0:T(8,128)} %bitcast.111) | data formatting | bytes 12582912 | tf_op jit(solution)/shard_map/all_to_all | solution.py:94
  166.8 13.4 %convolution_bitcast_fusion = f32[3,384,64,32]{1,2,3,0:T(8,128)S(1)} fusion(f32[384,256,1,1]{1,0,3,2:T(8,128)S(1)} %copy-done.8, f32[3,256,64,32]{1,2,3,0:T(8,128)} %copy.94), kind=kOutput, calls=%fused_computation.19 | convolution fusion | flops 7247757312 | bytes 16121856 | tf_op jit(solution)/shard_map/jk,fkpe->fjpe/dot_general | solution.py:95
  180.2 3.7 slice_bitcast_fusion.2
  183.9 2.9 copy-done
  186.7 11.6 %fusion.16 = f32[3,384,32,64]{1,3,2,0:T(8,128)} fusion(f32[3,384,64,32]{1,2,3,0:T(8,128)S(1)} %convolution_bitcast_fusion, f32[64,64,1,1]{1,0,3,2:T(8,128)S(1)} %copy-done.12), kind=kOutput, calls=%fused_computation.56 | convolution fusion | flops 1811939328 | bytes 18890752 | tf_op jit(solution)/shard_map/qp,fjpe->fjqe/dot_general | solution.py:99
  198.4 12.5 %fusion.17 = f32[384,3,64,32]{0,2,3,1:T(8,128)} fusion(f32[384,256,1,1]{1,0,3,2:T(8,128)S(1)} %copy-done.7, f32[3,256,64,32]{1,2,3,0:T(8,128)S(1)} %bitcast.109), kind=kOutput, calls=%fused_computation.57 | convolution fusion | flops 7247757312 | bytes 16121856 | tf_op jit(solution)/shard_map/jk,fkpe->fjpe/dot_general | solution.py:97
  210.9 22.2 %fusion = f32[3,384,64,32]{1,2,3,0:T(8,128)} fusion(f32[3,384,32,64]{1,3,2,0:T(8,128)} %fusion.16, f32[384,3,64,32]{0,2,3,1:T(8,128)} %fusion.17, f32[384,64,32]{0,1,2:T(8,128)} %get-tuple-element.23, f32[64,32]{0,1:T(8,128)S(1)} %copy.98, f32[64,32]{0,1:T(8,128)S(1)} %copy.97, f32[384,64,32]{0,1,2:T(8,128)} %get-tuple-element.24, f32[64,32]{0,1:T(8,128)S(1)} %copy.96, ...), kind=kOutput, calls=%fused_computation.5 | convolution fusion | flops 1840250880 | bytes 47235072 | tf_op jit(solution)/shard_map/qp,fjpe->fjqe/dot_general | solution.py:100
  233.1 18.4 %fusion.6 = f32[3,64,32,256]{3,2,1,0:T(8,128)S(1)} fusion(f32[256,384,1,1]{1,0,3,2:T(8,128)} %constant.107, f32[3,384,64,32]{1,2,3,0:T(8,128)} %fusion), kind=kOutput, calls=%fused_computation.15 | convolution fusion | flops 7247757312 | bytes 16121856 | tf_op jit(solution)/shard_map/kj,fjpe->fkpe/dot_general | solution.py:104
  251.5 12.0 %dynamic-slice_bitcast_fusion = (f32[3,32,64,32]{1,3,2,0:T(8,128)}, f32[3,32,64,32]{1,3,2,0:T(8,128)}, f32[3,32,64,32]{1,3,2,0:T(8,128)}, f32[3,32,64,32]{1,3,2,...) fusion(f32[3,64,32,256]{3,2,1,0:T(8,128)S(1)} %fusion.6, ...), kind=kLoop, calls=%fused_computation.23 | loop fusion | bytes 12582944 | tf_op jit(solution)/shard_map/dynamic_slice | solution.py:113
  263.5 4.0 copy.102
  267.5 2.6 broadcast_multiply_fusion
  270.1 3.8 copy.104
  274.5 2.6 copy.106
  278.4 9.3 %copy.133 = f32[64,64,256,1]{1,0,3,2:T(8,128)} copy(f32[64,64,256,1]{2,1,0,3:T(8,128)} %bitcast.118) | data formatting | bytes 8388608 | tf_op args[3]
  288.0 2.4 copy.101
  290.4 4.0 copy.108
  294.9 3.8 copy.110
  299.8 3.8 copy.112
  303.7 3.0 copy.114
  306.7 6.1 %broadcast_in_dim.15 = f32[3,32,64,256]{2,1,0,3:T(8,128)} broadcast(f32[]{:T(128)} %constant.71.clone.1), dimensions={} | broadcast | bytes 6291460 | tf_op jit(solution)/shard_map/broadcast_in_dim | solution.py:111
  314.6 3.5 copy_dynamic-update-slice_fusion.6
  318.1 2.1 collective-permute-start.6
  320.3 3.5 copy_dynamic-update-slice_fusion.5
  323.8 20.5 %collective-permute-done.2 = f32[3,32,64,32]{2,3,1,0:T(8,128)} collective-permute-done((f32[3,32,64,32]{2,3,1,0:T(8,128)}, f32[3,32,64,32]{2,3,1,0:T(8,128)}, u32[]{:S(2)}, u32[]{:S(2)}) %collective-permute-start.2) | collective-permute-done | bytes 786464 | tf_op jit(solution)/shard_map/ppermute | solution.py:115
  344.4 3.5 copy_dynamic-update-slice_fusion.4
  347.9 3.5 copy_dynamic-update-slice_fusion.3
  351.3 80.4 %collective-permute-done.4 = f32[3,32,64,32]{2,3,1,0:T(8,128)} collective-permute-done((f32[3,32,64,32]{2,3,1,0:T(8,128)}, f32[3,32,64,32]{2,3,1,0:T(8,128)}, u32[]{:S(2)}, u32[]{:S(2)}) %collective-permute-start.4) | collective-permute-done | bytes 786464 | tf_op jit(solution)/shard_map/ppermute | solution.py:115
  431.7 3.5 copy_dynamic-update-slice_fusion.2
  435.2 2.0 copy_dynamic-update-slice_fusion.1
  437.3 2.1 copy_dynamic-update-slice_fusion
  439.4 35.7 %bitcast_add_fusion = f32[3,32,64,256]{2,1,0,3:T(8,128)} fusion(f32[32,64,256]{1,0,2:T(8,128)} %broadcast_multiply_fusion, f32[3,32,64,256]{2,1,0,3:T(8,128)} %copy.116, f32[3,32,64,256]{2,1,0,3:T(8,128)} %copy_dynamic-update-slice_fusion, f32[64,64,256,1]{1,0,3,2:T(8,128)} %copy.133), kind=kOutput, calls=%fused_computation.3 | convolution fusion | flops 1214251008 | bytes 25165824 | tf_op jit(solution)/shard_map/ije,fkje->fkie/dot_general | solution.py:122
  475.1 12.1 %copy.120 = f32[3,32,64,256]{3,1,0,2:T(8,128)} copy(f32[3,32,64,256]{2,1,0,3:T(8,128)} %bitcast_add_fusion) | data formatting | bytes 12582912 | tf_op jit(solution)/shard_map/add | solution.py:123
  487.2 3.5 gather_fusion
  490.7 10.0 %copy.138 = f32[256,28,3,32]{3,2,1,0:T(4,128)} copy(f32[256,28,3,32]{0,3,2,1:T(8,128)S(1)} %bitcast.113) | data formatting | bytes 5505024 | tf_op jit(solution)/shard_map/reshape | solution.py:126
  500.7 14.7 %reshape.111 = f32[7168,96]{1,0:T(8,128)} reshape(f32[256,28,3,32]{3,2,1,0:T(4,128)} %copy.138) | data formatting | bytes 5505024 | tf_op jit(solution)/shard_map/reshape | solution.py:126
  515.4 39.3 %scatter_custom_fusion = f32[3456,96]{1,0:T(8,128)S(1)} fusion(s32[7168]{0:T(1024)S(1)} %reshape.95, f32[7168,96]{1,0:T(8,128)} %reshape.111, f32[]{:T(128)} %constant.71.clone.1), kind=kCustom, calls=%fused_computation.41 | custom fusion | flops 688128 | bytes 1327616 | tf_op jit(solution)/shard_map/scatter-add | solution.py:128
  555.3 4.3 collective-permute-start.7
  561.4 4.2 collective-permute-start.8
  566.9 11.2 %copy.127 = f32[3,32,64,256]{3,2,1,0:T(8,128)} copy(f32[3,32,64,256]{2,1,0,3:T(8,128)} %bitcast_add_fusion) | data formatting | bytes 12582912
  581.9 3.2 gather_fusion.1
  585.0 9.8 %convolution_bitcast_fusion.1 = f32[96,26,128]{2,0,1:T(8,128)S(1)} fusion(f32[96,26,4,128]{3,0,2,1:T(8,128)} %bitcast.112, f32[26,4,128,128]{3,2,1,0:T(8,128)} %param.23), kind=kOutput, calls=%fused_computation.40 | convolution fusion | flops 1962934272 | bytes 13205504 | tf_op jit(solution)/shard_map/rsab,frsb->fra/dot_general | solution.py:139
  (80 shorter events, 16.1 us)
Async XLA Ops:
  26.0 5.3 copy-start.10
  26.0 5.7 copy-start.9
  26.0 5.9 copy-start.16
  26.0 77.1 %all-to-all-start = ((f32[8,1,196608]{2,1,0:T(1,128)}), f32[8,1,196608]{2,1,0:T(1,128)}, u32[]{:S(2)}, u32[]{:S(2)}) async-start(f32[8,1,196608]{2,1,0:T(1,128)} %reshape.114), calls=%async_computation | async-start | bytes 12582912 | tf_op jit(solution)/shard_map/all_to_all | solution.py:94
  155.7 11.0 %copy-start.8 = (f32[384,256,1,1]{1,0,3,2:T(8,128)S(1)}, f32[384,256,1,1]{1,0,3,2:T(8,128)}, u32[]{:S(2)}) copy-start(f32[384,256,1,1]{1,0,3,2:T(8,128)} %constant.103) | copy-start | bytes 1179652
  180.2 6.6 %copy-start = (f32[3,384,64,32]{1,2,3,0:T(8,128)}, f32[3,384,64,32]{1,2,3,0:T(8,128)S(1)}, u32[]{:S(2)}) copy-start(f32[3,384,64,32]{1,2,3,0:T(8,128)S(1)} %convolution_bitcast_fusion) | copy-start | bytes 28311556
  180.2 6.6 %copy-start.12 = (f32[64,64,1,1]{1,0,3,2:T(8,128)S(1)}, f32[64,64,1,1]{1,0,3,2:T(8,128)}, u32[]{:S(2)}) copy-start(f32[64,64,1,1]{1,0,3,2:T(8,128)} %constant.104) | copy-start | bytes 49156
  180.2 18.2 %slice-start = ((s8[6291456]{0:T(1024)(128)(4,1)}), s8[4194304]{0:T(1024)(128)(4,1)S(1)}, s32[]{:S(2)}) async-start(s8[6291456]{0:T(1024)(128)(4,1)} %bitcast.108), calls=%async_computation.1 | async-start | bytes 8388608
  186.7 11.6 %slice-start.1 = ((s8[6291456]{0:T(1024)(128)(4,1)}), s8[2097152]{0:T(1024)(128)(4,1)S(1)}, s32[]{:S(2)}) async-start(s8[6291456]{0:T(1024)(128)(4,1)} %bitcast.108), calls=%async_computation.2 | async-start | bytes 4194304
  186.7 11.6 %copy-start.7 = (f32[384,256,1,1]{1,0,3,2:T(8,128)S(1)}, f32[384,256,1,1]{1,0,3,2:T(8,128)}, u32[]{:S(2)}) copy-start(f32[384,256,1,1]{1,0,3,2:T(8,128)} %constant.106) | copy-start | bytes 1179652
  198.4 12.5 %copy-start.11 = (f32[64,64,1,1]{1,0,3,2:T(8,128)S(1)}, f32[64,64,1,1]{1,0,3,2:T(8,128)}, u32[]{:S(2)}) copy-start(f32[64,64,1,1]{1,0,3,2:T(8,128)} %constant.105) | copy-start | bytes 49156
  263.4 11.0 %copy-start.13 = (s32[256,28]{0,1:T(8,128)S(1)}, s32[256,28]{0,1:T(8,128)}, u32[]{:S(2)}) copy-start(s32[256,28]{0,1:T(8,128)} %param.21) | copy-start | bytes 86020
  263.4 11.0 %copy-start.3 = (f32[3,32,64,32]{1,3,2,0:T(8,128)S(1)}, f32[3,32,64,32]{1,3,2,0:T(8,128)}, u32[]{:S(2)}) copy-start(f32[3,32,64,32]{1,3,2,0:T(8,128)} %get-tuple-element.29) | copy-start | bytes 2359300
  267.5 11.0 %copy-start.15 = (s32[28]{0:T(128)S(1)}, s32[28]{0:T(128)}, u32[]{:S(2)}) copy-start(s32[28]{0:T(128)} %constant.102) | copy-start | bytes 340
  267.5 46.6 %collective-permute-start = (f32[3,32,64,32]{2,3,1,0:T(8,128)}, f32[3,32,64,32]{2,3,1,0:T(8,128)}, u32[]{:S(2)}, u32[]{:S(2)}) collective-permute-start(f32[3,32,64,32]{2,3,1,0:T(8,128)} %copy.102), channel_id=1, source_target_pairs={{0,4},{4,0},{8,12},{12,8},{16,20},{20,16},{24,28},{28,24},{1,5},{5... | collective-permute-start | bytes 2359304 | tf_op jit(solution)/shard_map/ppermute | solution.py:115
  273.9 44.2 %collective-permute-start.1 = (f32[3,32,64,32]{2,3,1,0:T(8,128)}, f32[3,32,64,32]{2,3,1,0:T(8,128)}, u32[]{:S(2)}, u32[]{:S(2)}) collective-permute-start(f32[3,32,64,32]{2,3,1,0:T(8,128)} %copy.104), channel_id=1, source_target_pairs={{0,8},{4,12},{8,0},{12,4},{16,24},{20,28},{24,16},{28,20},{1,9},{5... | collective-permute-start | bytes 2359304 | tf_op jit(solution)/shard_map/ppermute | solution.py:115
  277.1 67.3 %collective-permute-start.2 = (f32[3,32,64,32]{2,3,1,0:T(8,128)}, f32[3,32,64,32]{2,3,1,0:T(8,128)}, u32[]{:S(2)}, u32[]{:S(2)}) collective-permute-start(f32[3,32,64,32]{2,3,1,0:T(8,128)} %copy.106), channel_id=1, source_target_pairs={{0,12},{4,8},{8,4},{12,0},{16,28},{20,24},{24,20},{28,16},{1,13},{... | collective-permute-start | bytes 2359304 | tf_op jit(solution)/shard_map/ppermute | solution.py:115
  278.4 9.6 %copy-start.2 = (f32[3,32,64,32]{1,3,2,0:T(8,128)S(1)}, f32[3,32,64,32]{1,3,2,0:T(8,128)}, u32[]{:S(2)}) copy-start(f32[3,32,64,32]{1,3,2,0:T(8,128)} %get-tuple-element.32) | copy-start | bytes 2359300
  290.4 13.3 %copy-start.1 = (f32[3,32,64,32]{1,3,2,0:T(8,128)S(1)}, f32[3,32,64,32]{1,3,2,0:T(8,128)}, u32[]{:S(2)}) copy-start(f32[3,32,64,32]{1,3,2,0:T(8,128)} %get-tuple-element.25) | copy-start | bytes 2359300
  294.4 53.5 %collective-permute-start.3 = (f32[3,32,64,32]{2,3,1,0:T(8,128)}, f32[3,32,64,32]{2,3,1,0:T(8,128)}, u32[]{:S(2)}, u32[]{:S(2)}) collective-permute-start(f32[3,32,64,32]{2,3,1,0:T(8,128)} %copy.108), channel_id=1, source_target_pairs={{0,16},{4,20},{8,24},{12,28},{16,0},{20,4},{24,8},{28,12},{1,17},{... | collective-permute-start | bytes 2359304 | tf_op jit(solution)/shard_map/ppermute | solution.py:115
  298.7 133.0 %collective-permute-start.4 = (f32[3,32,64,32]{2,3,1,0:T(8,128)}, f32[3,32,64,32]{2,3,1,0:T(8,128)}, u32[]{:S(2)}, u32[]{:S(2)}) collective-permute-start(f32[3,32,64,32]{2,3,1,0:T(8,128)} %copy.110), channel_id=1, source_target_pairs={{0,20},{4,16},{8,28},{12,24},{16,4},{20,0},{24,12},{28,8},{1,21},{... | collective-permute-start | bytes 2359304 | tf_op jit(solution)/shard_map/ppermute | solution.py:115
  306.7 6.1 %copy-start.4 = (f32[3,32,64,32]{2,1,0,3:T(8,128)S(1)}, f32[3,32,64,32]{2,1,0,3:T(8,128)}, u32[]{:S(2)}) copy-start(f32[3,32,64,32]{2,1,0,3:T(8,128)} %copy.101) | copy-start | bytes 2359300
  306.7 7.4 %copy-start.6 = (f32[3,32,64,32]{2,3,1,0:T(8,128)S(1)}, f32[3,32,64,32]{2,3,1,0:T(8,128)}, u32[]{:S(2)}) copy-start(f32[3,32,64,32]{2,3,1,0:T(8,128)} %copy.112) | copy-start | bytes 2359300
  312.8 5.3 copy-start.5
  314.1 121.2 %collective-permute-start.5 = (f32[3,32,64,32]{2,3,1,0:T(8,128)S(1)}, f32[3,32,64,32]{2,3,1,0:T(8,128)S(1)}, u32[]{:S(2)}, u32[]{:S(2)}) collective-permute-start(f32[3,32,64,32]{2,3,1,0:T(8,128)S(1)} %copy-done.6), channel_id=1, source_target_pairs={{0,24},{4,28},{8,16},{12,20},{16,8},{20,12},{24,0},{28,4},{1,25},{... | collective-permute-start | bytes 2359304 | tf_op jit(solution)/shard_map/ppermute | solution.py:115
  318.1 119.2 %collective-permute-start.6 = (f32[3,32,64,32]{2,3,1,0:T(8,128)S(1)}, f32[3,32,64,32]{2,3,1,0:T(8,128)S(1)}, u32[]{:S(2)}, u32[]{:S(2)}) collective-permute-start(f32[3,32,64,32]{2,3,1,0:T(8,128)S(1)} %copy-done.5), channel_id=1, source_target_pairs={{0,28},{4,24},{8,20},{12,16},{16,12},{20,8},{24,4},{28,0},{1,29},{... | collective-permute-start | bytes 2359304 | tf_op jit(solution)/shard_map/ppermute | solution.py:115
  500.7 58.9 %copy-start.14 = (s32[26,4]{0,1:T(4,128)S(1)}, s32[26,4]{0,1:T(4,128)}, u32[]{:S(2)}) copy-start(s32[26,4]{0,1:T(4,128)} %param.22) | copy-start | bytes 1252
  555.3 6.1 %collective-permute-start.7 = (f32[3,32,128]{2,1,0:T(8,128)S(1)}, f32[3,32,128]{2,1,0:T(8,128)S(1)}, u32[]{:S(2)}, u32[]{:S(2)}) collective-permute-start(f32[3,32,128]{2,1,0:T(8,128)S(1)} %slice.79), channel_id=1, source_target_pairs={{0,1},{1,2},{2,3},{4,5},{5,6},{6,7},{8,9},{9,10},{10,11},{12,13},{... | collective-permute-start | bytes 147464 | tf_op jit(solution)/shard_map/ppermute | solution.py:26
  561.4 16.8 %collective-permute-start.8 = (f32[3,32,256]{2,1,0:T(8,128)S(1)}, f32[3,32,256]{2,1,0:T(8,128)S(1)}, u32[]{:S(2)}, u32[]{:S(2)}) collective-permute-start(f32[3,32,256]{2,1,0:T(8,128)S(1)} %get-tuple-element.33), channel_id=1, source_target_pairs={{0,1},{1,2},{2,3},{4,5},{5,6},{6,7},{8,9},{9,10},{10,11},{12,13},{... | collective-permute-start | bytes 294920 | tf_op jit(solution)/shard_map/ppermute | solution.py:36
  565.6 12.5 %collective-permute-start.9 = (f32[3,32,256]{2,1,0:T(8,128)S(1)}, f32[3,32,256]{2,1,0:T(8,128)S(1)}, u32[]{:S(2)}, u32[]{:S(2)}) collective-permute-start(f32[3,32,256]{2,1,0:T(8,128)S(1)} %get-tuple-element.34), channel_id=1, source_target_pairs={{1,0},{2,1},{3,2},{5,4},{6,5},{7,6},{9,8},{10,9},{11,10},{13,12},{... | collective-permute-start | bytes 294920 | tf_op jit(solution)/shard_map/ppermute | solution.py:37
